TPU v7x, 32 devices: a whole 2x2x4 slice. The times are simulated.
32 devices in a mesh: grp: 2 (over y), seq: 16 (over z, x, core).
Axes of the slice: x: 2, y: 2, z: 4, core: 2. Of those that a mesh axis runs over, the one named last changes fastest.
Arguments:
- queries: bfloat16 [8192, 2048], P(('grp', 'seq')), parts along dimension 0, may hold values from -6 to 6
- keys: bfloat16 [8192, 2048], P(('grp', 'seq')), parts along dimension 0, may hold values from -6 to 6
- values: bfloat16 [8192, 2048], P(('grp', 'seq')), parts along dimension 0, may hold values from -6 to 6
- feature_map: bfloat16 [16, 128, 128], replicated, may hold values from -0.5 to 0.5
- out_grad: bfloat16 [8192, 2048], P(('grp', 'seq')), parts along dimension 0, may hold values from -6 to 6
Outputs:
- attended: bfloat16 [8192, 2048], P(('grp', 'seq')), parts along dimension 0
- query_grad: bfloat16 [8192, 2048], P(('grp', 'seq')), parts along dimension 0
- key_grad: bfloat16 [8192, 2048], P(('grp', 'seq')), parts along dimension 0
- value_grad: bfloat16 [8192, 2048], P(('grp', 'seq')), parts along dimension 0
- feature_grad: float32 [524288], P(('grp', 'seq')), parts along dimension 0
There are 2 independent parts, one for each index of `grp`. A program takes and returns all parts, laid end to end along the dimension named above; an argument that names none is the same for every part. Nothing has to cross between parts.
All inputs are finite; a program needn't handle non-finite values.
Results may differ from a plain program's by a relative error of at most 0.0085.
Values may be sent and summed in bfloat16 or wider, within the bound.
A program may use at most 64 MiB of HBM per device.

v0:
```python
import math

import jax
import jax.numpy as jnp
from jax import lax
from jax.sharding import PartitionSpec as P


def shifted(value, axis, steps):
    count = lax.axis_size(axis)
    initial, last = (max(0, -steps), min(count, count - steps))
    return lax.ppermute(value, axis, [(source, source + steps) for source in range(initial, last)])


def features(inputs, weight):
    lifted = jnp.einsum("thd,hde->the", inputs, weight, preferred_element_type=jnp.float32)
    mapped = jnp.where(lifted > 0, lifted + 1.0, jnp.exp(jnp.minimum(lifted, 0.0)))
    return (lifted, mapped.astype(jnp.bfloat16))


def slope_of(lifted):
    return jnp.where(lifted > 0, 1.0, jnp.exp(jnp.minimum(lifted, 0.0)))


def earlier_sum(state):
    levels = lax.axis_size("seq").bit_length() - 1
    running = state
    for level in range(levels):
        running = running + shifted(running, "seq", 1 << level)
    return running - state


def later_sum(state):
    levels = lax.axis_size("seq").bit_length() - 1
    running = state
    for level in range(levels):
        running = running + shifted(running, "seq", -(1 << level))
    return running - state


def local_forward(feat_q, feat_k, value_heads, prefix, causal):
    scores = jnp.einsum("the,she->hts", feat_q, feat_k, preferred_element_type=jnp.float32)
    scores = jnp.where(causal, scores, 0.0).astype(jnp.bfloat16)
    numerator = jnp.einsum("hts,shf->thf", scores, value_heads, preferred_element_type=jnp.float32)
    numerator = numerator + jnp.einsum(
        "the,hef->thf", feat_q, prefix.astype(jnp.bfloat16), preferred_element_type=jnp.float32
    )
    return (numerator, scores)


def local(queries, keys, values, feature_map, out_grad):
    token_count = queries.shape[0]
    head_count = feature_map.shape[0]
    head_size = feature_map.shape[1]
    shaped = (token_count, head_count, head_size)
    query_heads = queries.reshape(shaped)
    key_heads = keys.reshape(shaped)
    value_heads = values.reshape(shaped)
    token_ids = lax.broadcasted_iota(jnp.int32, (token_count, token_count), 0)
    other_ids = lax.broadcasted_iota(jnp.int32, (token_count, token_count), 1)
    causal = (token_ids >= other_ids)[None, :, :]
    lifted_q, feat_q = features(query_heads, feature_map)
    lifted_k, feat_k = features(key_heads, feature_map)
    block_state = jnp.einsum(
        "the,thf->hef", feat_k, value_heads, preferred_element_type=jnp.float32
    )
    prefix = earlier_sum(block_state)
    numerator, scores = local_forward(feat_q, feat_k, value_heads, prefix, causal)
    recip = lax.rsqrt(jnp.mean(numerator * numerator, axis=-1, keepdims=True) + 1e-06)
    attended = (numerator * recip).astype(jnp.bfloat16)
    upstream = out_grad.reshape(shaped).astype(jnp.float32)
    inner = jnp.mean(upstream * numerator, axis=-1, keepdims=True)
    grad_numer = (recip * (upstream - numerator * recip * recip * inner)).astype(jnp.bfloat16)
    local_adjoint = jnp.einsum(
        "the,thf->hef", feat_q, grad_numer, preferred_element_type=jnp.float32
    )
    suffix = later_sum(local_adjoint)
    back_scores = jnp.einsum(
        "thf,shf->hts", grad_numer, value_heads, preferred_element_type=jnp.float32
    )
    back_scores = jnp.where(causal, back_scores, 0.0).astype(jnp.bfloat16)
    prefix_low = prefix.astype(jnp.bfloat16)
    suffix_low = suffix.astype(jnp.bfloat16)
    grad_fq = jnp.einsum("hts,she->the", back_scores, feat_k, preferred_element_type=jnp.float32)
    grad_fq = grad_fq + jnp.einsum(
        "thf,hef->the", grad_numer, prefix_low, preferred_element_type=jnp.float32
    )
    grad_fk = jnp.einsum("hts,the->she", back_scores, feat_q, preferred_element_type=jnp.float32)
    grad_fk = grad_fk + jnp.einsum(
        "shf,hef->she", value_heads, suffix_low, preferred_element_type=jnp.float32
    )
    value_grad = jnp.einsum("hts,thf->shf", scores, grad_numer, preferred_element_type=jnp.float32)
    value_grad = (
        value_grad
        + jnp.einsum("she,hef->shf", feat_k, suffix_low, preferred_element_type=jnp.float32)
    ).astype(jnp.bfloat16)
    grad_qa = (grad_fq * slope_of(lifted_q)).astype(jnp.bfloat16)
    grad_ka = (grad_fk * slope_of(lifted_k)).astype(jnp.bfloat16)
    query_grad = jnp.einsum(
        "the,hde->thd", grad_qa, feature_map, preferred_element_type=jnp.float32
    ).astype(jnp.bfloat16)
    key_grad = jnp.einsum(
        "the,hde->thd", grad_ka, feature_map, preferred_element_type=jnp.float32
    ).astype(jnp.bfloat16)
    weight_term = jnp.einsum(
        "thd,the->hde", query_heads, grad_qa, preferred_element_type=jnp.float32
    )
    weight_term = weight_term + jnp.einsum(
        "thd,the->hde", key_heads, grad_ka, preferred_element_type=jnp.float32
    )
    total_tokens = token_count * lax.axis_size("seq")
    weight_term = weight_term * (1.0 / math.sqrt(total_tokens))
    feature_grad = lax.psum_scatter(
        weight_term.reshape(head_count * head_size * head_size),
        "seq",
        scatter_dimension=0,
        tiled=True,
    )
    flat = (token_count, head_count * head_size)
    return (
        attended.reshape(flat),
        query_grad.reshape(flat),
        key_grad.reshape(flat),
        value_grad.reshape(flat),
        feature_grad,
    )


def solution(mesh):
    in_specs = (
        P(("grp", "seq"), None),
        P(("grp", "seq"), None),
        P(("grp", "seq"), None),
        P(),
        P(("grp", "seq"), None),
    )
    out_specs = (
        P(("grp", "seq"), None),
        P(("grp", "seq"), None),
        P(("grp", "seq"), None),
        P(("grp", "seq"), None),
        P(("grp", "seq")),
    )
    return jax.shard_map(local, mesh=mesh, in_specs=in_specs, out_specs=out_specs, check_vma=False)
```

profile of v0, /device:TPU:0, one launch (start us, length us, event | category | flops | bytes accessed | tf_op | source)
XLA Modules:
  0.0 363.0 jit_solution(10282948561593231518)
XLA Ops:
  7.2 1.9 fusion.13
  10.5 2.4 collective-permute-start
  13.0 2.2 collective-permute-done
  15.3 16.5 %collective-permute-start.1 = (f32[16,128,128]{2,1,0:T(8,128)S(1)}, f32[16,128,128]{2,1,0:T(8,128)S(1)}, u32[]{:S(2)}, u32[]{:S(2)}) collective-permute-start(f32[16,128,128]{2,1,0:T(8,128)S(1)} %add.66), channel_id=1, source_target_pairs={{0,2},{1,3},{2,4},{3,5},{4,6},{5,7},{6,8},{7,9},{8,10},{9,11},{10,... | collective-permute-start | bytes 3145736 | tf_op jit(solution)/shard_map/ppermute | solution.py:12
  31.8 21.7 %collective-permute-done.1 = f32[16,128,128]{2,1,0:T(8,128)S(1)} collective-permute-done((f32[16,128,128]{2,1,0:T(8,128)S(1)}, f32[16,128,128]{2,1,0:T(8,128)S(1)}, u32[]{:S(2)}, u32[]{:S(2)}) %collective-permute-start.1) | collective-permute-done | bytes 1048608 | tf_op jit(solution)/shard_map/ppermute | solution.py:12
  53.7 5.4 %collective-permute-start.2 = (f32[16,128,128]{2,1,0:T(8,128)S(1)}, f32[16,128,128]{2,1,0:T(8,128)S(1)}, u32[]{:S(2)}, u32[]{:S(2)}) collective-permute-start(f32[16,128,128]{2,1,0:T(8,128)S(1)} %add.67), channel_id=1, source_target_pairs={{0,4},{1,5},{2,6},{3,7},{4,8},{5,9},{6,10},{7,11},{8,12},{9,13},{1... | collective-permute-start | bytes 3145736 | tf_op jit(solution)/shard_map/ppermute | solution.py:12
  59.1 1.9 fusion.17
  60.9 17.9 %collective-permute-done.2 = f32[16,128,128]{2,1,0:T(8,128)S(1)} collective-permute-done((f32[16,128,128]{2,1,0:T(8,128)S(1)}, f32[16,128,128]{2,1,0:T(8,128)S(1)}, u32[]{:S(2)}, u32[]{:S(2)}) %collective-permute-start.2) | collective-permute-done | bytes 1048608 | tf_op jit(solution)/shard_map/ppermute | solution.py:12
  80.0 6.4 %collective-permute-start.3 = (f32[16,128,128]{2,1,0:T(8,128)}, f32[16,128,128]{2,1,0:T(8,128)}, u32[]{:S(2)}, u32[]{:S(2)}) collective-permute-start(f32[16,128,128]{2,1,0:T(8,128)} %add.68), channel_id=1, source_target_pairs={{0,8},{1,9},{2,10},{3,11},{4,12},{5,13},{6,14},{7,15},{16,24},{17,... | collective-permute-start | bytes 3145736 | tf_op jit(solution)/shard_map/ppermute | solution.py:12
  88.1 2.1 fusion.4
  92.3 12.4 %collective-permute-done.3 = f32[16,128,128]{2,1,0:T(8,128)} collective-permute-done((f32[16,128,128]{2,1,0:T(8,128)}, f32[16,128,128]{2,1,0:T(8,128)}, u32[]{:S(2)}, u32[]{:S(2)}) %collective-permute-start.3) | collective-permute-done | bytes 1048608 | tf_op jit(solution)/shard_map/ppermute | solution.py:12
  110.7 3.3 collective-permute-done.4
  117.7 24.7 %collective-permute-done.5 = f32[16,128,128]{2,1,0:T(8,128)} collective-permute-done((f32[16,128,128]{2,1,0:T(8,128)}, f32[16,128,128]{2,1,0:T(8,128)}, u32[]{:S(2)}, u32[]{:S(2)}) %collective-permute-start.5) | collective-permute-done | bytes 1048608 | tf_op jit(solution)/shard_map/ppermute | solution.py:12
  149.3 54.2 %collective-permute-done.6 = f32[16,128,128]{2,1,0:T(8,128)S(1)} collective-permute-done((f32[16,128,128]{2,1,0:T(8,128)S(1)}, f32[16,128,128]{2,1,0:T(8,128)S(1)}, u32[]{:S(2)}, u32[]{:S(2)}) %collective-permute-start.6) | collective-permute-done | bytes 1048608 | tf_op jit(solution)/shard_map/ppermute | solution.py:12
  207.5 2.3 copy.86
  209.8 2.3 copy.87
  212.0 2.1 fusion.15
  214.5 1.8 fusion.30
  217.0 38.4 %collective-permute-done.7 = f32[16,128,128]{2,1,0:T(8,128)} collective-permute-done((f32[16,128,128]{2,1,0:T(8,128)}, f32[16,128,128]{2,1,0:T(8,128)}, u32[]{:S(2)}, u32[]{:S(2)}) %collective-permute-start.7) | collective-permute-done | bytes 1048608 | tf_op jit(solution)/shard_map/ppermute | solution.py:12
  260.0 2.5 copy.85
  262.5 3.2 add_convert_fusion
  265.8 2.3 copy.89
  269.5 2.3 copy.88
  271.8 82.9 %all-reduce.3.cloned.1.call-done = f32[262144]{0:T(1024)} async-done(((f32[262144]{0:T(1024)}), f32[262144]{0:T(1024)}) %all-reduce.3.cloned.1.call-update) | async-done | bytes 1048592
  (88 shorter events, 34.9 us)
Async XLA Ops:
  7.2 2.5 copy-start
  7.2 347.5 %all-reduce.3.cloned.1.call-start = ((), (), s32[]{:S(2)}) async-start(), calls=%async_computation | async-start | bytes 2097152
  10.5 43.1 %copy-start.12 = (f32[16,128,128]{2,1,0:T(8,128)}, f32[16,128,128]{2,1,0:T(8,128)S(1)}, u32[]{:S(2)}) copy-start(f32[16,128,128]{2,1,0:T(8,128)S(1)} %fusion.10) | copy-start | bytes 3145732
  10.5 4.6 %collective-permute-start = (f32[16,128,128]{2,1,0:T(8,128)S(1)}, f32[16,128,128]{2,1,0:T(8,128)S(1)}, u32[]{:S(2)}, u32[]{:S(2)}) collective-permute-start(f32[16,128,128]{2,1,0:T(8,128)S(1)} %fusion.10), channel_id=1, source_target_pairs={{0,1},{1,2},{2,3},{3,4},{4,5},{5,6},{6,7},{7,8},{8,9},{9,10},{10,1... | collective-permute-start | bytes 3145736 | tf_op jit(solution)/shard_map/ppermute | solution.py:12
  15.3 43.8 %copy-start.15 = (bf16[16,128,128]{2,1,0:T(8,128)(2,1)S(1)}, bf16[16,128,128]{2,1,0:T(8,128)(2,1)}, u32[]{:S(2)}) copy-start(bf16[16,128,128]{2,1,0:T(8,128)(2,1)} %param.8) | copy-start | bytes 1572868
  15.3 43.8 %copy-start.23 = (bf16[256,2048]{1,0:T(8,128)(2,1)S(1)}, bf16[256,2048]{1,0:T(8,128)(2,1)}, u32[]{:S(2)}) copy-start(bf16[256,2048]{1,0:T(8,128)(2,1)} %param.5) | copy-start | bytes 3145732
  15.3 38.2 %collective-permute-start.1 = (f32[16,128,128]{2,1,0:T(8,128)S(1)}, f32[16,128,128]{2,1,0:T(8,128)S(1)}, u32[]{:S(2)}, u32[]{:S(2)}) collective-permute-start(f32[16,128,128]{2,1,0:T(8,128)S(1)} %add.66), channel_id=1, source_target_pairs={{0,2},{1,3},{2,4},{3,5},{4,6},{5,7},{6,8},{7,9},{8,10},{9,11},{10,... | collective-permute-start | bytes 3145736 | tf_op jit(solution)/shard_map/ppermute | solution.py:12
  53.7 25.2 %collective-permute-start.2 = (f32[16,128,128]{2,1,0:T(8,128)S(1)}, f32[16,128,128]{2,1,0:T(8,128)S(1)}, u32[]{:S(2)}, u32[]{:S(2)}) collective-permute-start(f32[16,128,128]{2,1,0:T(8,128)S(1)} %add.67), channel_id=1, source_target_pairs={{0,4},{1,5},{2,6},{3,7},{4,8},{5,9},{6,10},{7,11},{8,12},{9,13},{1... | collective-permute-start | bytes 3145736 | tf_op jit(solution)/shard_map/ppermute | solution.py:12
  60.9 25.5 %copy-start.25 = (bf16[256,2048]{1,0:T(8,128)(2,1)S(1)}, bf16[256,2048]{1,0:T(8,128)(2,1)}, u32[]{:S(2)}) copy-start(bf16[256,2048]{1,0:T(8,128)(2,1)} %param.9) | copy-start | bytes 3145732
  80.0 24.7 %collective-permute-start.3 = (f32[16,128,128]{2,1,0:T(8,128)}, f32[16,128,128]{2,1,0:T(8,128)}, u32[]{:S(2)}, u32[]{:S(2)}) collective-permute-start(f32[16,128,128]{2,1,0:T(8,128)} %add.68), channel_id=1, source_target_pairs={{0,8},{1,9},{2,10},{3,11},{4,12},{5,13},{6,14},{7,15},{16,24},{17,... | collective-permute-start | bytes 3145736 | tf_op jit(solution)/shard_map/ppermute | solution.py:12
  91.0 13.7 %copy-start.13 = (f32[16,128,128]{2,1,0:T(8,128)S(1)}, f32[16,128,128]{2,1,0:T(8,128)}, u32[]{:S(2)}) copy-start(f32[16,128,128]{2,1,0:T(8,128)} %copy-done.12) | copy-start | bytes 3145732
  92.3 14.1 %copy-start.6 = (f32[256,2048]{0,1:T(8,128)S(1)}, f32[256,2048]{0,1:T(8,128)}, u32[]{:S(2)}) copy-start(f32[256,2048]{0,1:T(8,128)} %copy.73) | copy-start | bytes 6291460
  108.8 6.3 %copy-start.7 = (bf16[256,16,128]{0,2,1:T(8,128)(2,1)}, bf16[256,16,128]{0,2,1:T(8,128)(2,1)S(1)}, u32[]{:S(2)}) copy-start(bf16[256,16,128]{0,2,1:T(8,128)(2,1)S(1)} %get-tuple-element.22) | copy-start | bytes 3145732
  109.3 7.1 %copy-start.10 = (f32[16,128,128]{2,1,0:T(8,128)}, f32[16,128,128]{2,1,0:T(8,128)S(1)}, u32[]{:S(2)}) copy-start(f32[16,128,128]{2,1,0:T(8,128)S(1)} %fusion.29) | copy-start | bytes 3145732
  109.3 7.1 %copy-start.26 = (u32[32]{0:T(128)S(1)}, u32[32]{0:T(128)}, u32[]{:S(2)}) copy-start(u32[32]{0:T(128)} %constant.16) | copy-start | bytes 388
  109.3 4.7 %collective-permute-start.4 = (f32[16,128,128]{2,1,0:T(8,128)S(1)}, f32[16,128,128]{2,1,0:T(8,128)S(1)}, u32[]{:S(2)}, u32[]{:S(2)}) collective-permute-start(f32[16,128,128]{2,1,0:T(8,128)S(1)} %fusion.29), channel_id=1, source_target_pairs={{1,0},{2,1},{3,2},{4,3},{5,4},{6,5},{7,6},{8,7},{9,8},{10,9},{11,1... | collective-permute-start | bytes 3145736 | tf_op jit(solution)/shard_map/ppermute | solution.py:12
  115.1 27.2 %collective-permute-start.5 = (f32[16,128,128]{2,1,0:T(8,128)}, f32[16,128,128]{2,1,0:T(8,128)}, u32[]{:S(2)}, u32[]{:S(2)}) collective-permute-start(f32[16,128,128]{2,1,0:T(8,128)} %add.74), channel_id=1, source_target_pairs={{2,0},{3,1},{4,2},{5,3},{6,4},{7,5},{8,6},{9,7},{10,8},{11,9},{12,... | collective-permute-start | bytes 3145736 | tf_op jit(solution)/shard_map/ppermute | solution.py:12
  117.6 27.6 %copy-start.8 = (bf16[256,16,128]{0,2,1:T(8,128)(2,1)S(1)}, bf16[256,16,128]{0,2,1:T(8,128)(2,1)}, u32[]{:S(2)}) copy-start(bf16[256,16,128]{0,2,1:T(8,128)(2,1)} %copy-done.7) | copy-start | bytes 3145732
  144.0 59.5 %collective-permute-start.6 = (f32[16,128,128]{2,1,0:T(8,128)S(1)}, f32[16,128,128]{2,1,0:T(8,128)S(1)}, u32[]{:S(2)}, u32[]{:S(2)}) collective-permute-start(f32[16,128,128]{2,1,0:T(8,128)S(1)} %add.75), channel_id=1, source_target_pairs={{4,0},{5,1},{6,2},{7,3},{8,4},{9,5},{10,6},{11,7},{12,8},{13,9},{1... | collective-permute-start | bytes 3145736 | tf_op jit(solution)/shard_map/ppermute | solution.py:12
  149.2 58.2 %copy-start.14 = (bf16[256,16,128]{0,2,1:T(8,128)(2,1)}, bf16[256,16,128]{0,2,1:T(8,128)(2,1)S(1)}, u32[]{:S(2)}) copy-start(bf16[256,16,128]{0,2,1:T(8,128)(2,1)S(1)} %fusion) | copy-start | bytes 3145732
  149.3 56.8 %copy-start.16 = (bf16[16,128,128]{2,1,0:T(8,128)(2,1)S(1)}, bf16[16,128,128]{2,1,0:T(8,128)(2,1)}, u32[]{:S(2)}) copy-start(bf16[16,128,128]{2,1,0:T(8,128)(2,1)} %param.8) | copy-start | bytes 1572868
  204.6 50.7 %collective-permute-start.7 = (f32[16,128,128]{2,1,0:T(8,128)}, f32[16,128,128]{2,1,0:T(8,128)}, u32[]{:S(2)}, u32[]{:S(2)}) collective-permute-start(f32[16,128,128]{2,1,0:T(8,128)} %add.76), channel_id=1, source_target_pairs={{8,0},{9,1},{10,2},{11,3},{12,4},{13,5},{14,6},{15,7},{24,16},{25,... | collective-permute-start | bytes 3145736 | tf_op jit(solution)/shard_map/ppermute | solution.py:12
  216.5 38.8 %copy-start.11 = (f32[16,128,128]{2,1,0:T(8,128)S(1)}, f32[16,128,128]{2,1,0:T(8,128)}, u32[]{:S(2)}) copy-start(f32[16,128,128]{2,1,0:T(8,128)} %copy-done.10) | copy-start | bytes 3145732
  217.0 40.1 %copy-start.2 = (f32[16,128,256]{2,1,0:T(8,128)S(1)}, f32[16,128,256]{2,1,0:T(8,128)}, u32[]{:S(2)}) copy-start(f32[16,128,256]{2,1,0:T(8,128)} %copy-done.1) | copy-start | bytes 6291460
  (12 other events, 20.9 us)
Sparse Core Ops, SparseCore 0:
  262.6 91.9 all-reduce.2
where the time goes:
time: 364 us; the launch traced here: 363 us
  waiting for transfers between devices  258 us (71%)
  starting transfers between devices  36.2 us (10%)
  matrix products  22 us (6%)
  local copies, waits for them, and re-layouts  19.2 us (5%)
  between operations  15.1 us (4%)
  other arithmetic  12.9 us (4%)
    ppermute x8, waiting for transfers between devices, shifted(): lax.ppermute(value, axis, [(source, source + steps) for source in range(i...  175 us
    unnamed x2, waiting for transfers between devices  82.9 us
    ppermute x8, starting transfers between devices, shifted(): lax.ppermute(value, axis, [(source, source + steps) for source in range(i...  36.2 us
    unnamed x60, local copies, waits for them, and re-layouts  15 us
  transfers between devices with their start and end apart: 9, of which 9 were waited for; matrix products, arithmetic and copies ran while one was open for 8% of the time, Pallas kernels for 0%

commit v1 on v0

v1 whole, which is shorter than its diff:
```python
import functools
import math

import jax
import jax.numpy as jnp
from jax import lax
from jax.experimental import pallas as pl
from jax.experimental.pallas import tpu as pltpu
from jax.sharding import PartitionSpec as P

MESH = pl.DeviceIdType.MESH
BF16 = jnp.bfloat16
F32 = jnp.float32


def mm(a, b, ca, cb):
    return lax.dot_general(a, b, (((ca,), (cb,)), ((), ())), preferred_element_type=F32)


def kernel(n, heads, dh, scale, q_ref, k_ref, v_ref, w_ref, y_ref,
           att_ref, qg_ref, kg_ref, vg_ref, fg_ref,
           fq_s, fk_s, a_s, num_s, gfk_s, vgl_s, wt_s, g_s,
           u_send, u_recv, p_send, p_buf, r_send, r_recv, s_send, q_buf, f_send, f_recv,
           send_sems, recv_sems):
    me = lax.axis_index("seq")
    rows = heads * dh // n
    cph = n // heads
    tokens = q_ref.shape[0]
    my_head = me // cph

    barrier = pltpu.get_barrier_semaphore()

    @pl.loop(1, n)
    def _(i):
        pl.semaphore_signal(barrier, inc=1, device_id={"seq": lax.rem(me + i, n)}, device_id_type=MESH)

    causal = (lax.broadcasted_iota(jnp.int32, (tokens, tokens), 0)
              >= lax.broadcasted_iota(jnp.int32, (tokens, tokens), 1))

    def cols(h):
        return pl.ds(pl.multiple_of(h * dh, dh), dh)

    def chunks(h):
        return pl.ds(h * cph, cph)

    def remote(phase, src, dst, to):
        return pltpu.make_async_remote_copy(
            src_ref=src.at[to], dst_ref=dst.at[me], send_sem=send_sems.at[phase],
            recv_sem=recv_sems.at[phase, me], device_id={"seq": to}, device_id_type=MESH)

    def send_chunk(phase, src, dst, to):
        @pl.when(to != me)
        def _():
            remote(phase, src, dst, to).start()

        @pl.when(to == me)
        def _():
            dst[me] = src[me]

    def send_head(phase, src, dst, h):
        @pl.loop(0, cph)
        def _(c):
            send_chunk(phase, src, dst, h * cph + c)

    def wait_chunk(phase, dst, j):
        @pl.when(j != me)
        def _():
            pltpu.make_async_remote_copy(
                src_ref=dst.at[j], dst_ref=dst.at[j], send_sem=send_sems.at[phase],
                recv_sem=recv_sems.at[phase, j], device_id={"seq": j}, device_id_type=MESH).wait_recv()

    def wait_head(phase, dst, h):
        @pl.loop(0, cph)
        def _(c):
            wait_chunk(phase, dst, h * cph + c)

    def features(lifted):
        return jnp.where(lifted > 0, lifted + 1.0, jnp.exp(jnp.minimum(lifted, 0.0))).astype(BF16)

    def slope_of(feat):
        return jnp.minimum(feat.astype(F32), 1.0)

    def head_of(buf, h):
        return buf[chunks(h)].reshape(dh, dh)

    def put_head(buf, h, value):
        buf[chunks(h)] = value.astype(BF16).reshape(cph, rows, dh)

    def state(h):
        c = cols(h)
        feat = features(mm(k_ref[:, c], w_ref[h], 1, 0))
        fk_s[:, c] = feat
        put_head(u_send, h, mm(feat, v_ref[:, c], 0, 0))

    state(lax.rem(my_head + 1, heads))
    pl.semaphore_wait(barrier, n - 1)
    send_head(0, u_send, u_recv, lax.rem(my_head + 1, heads))

    @pl.loop(2, heads + 1)
    def _(i):
        h = lax.rem(my_head + i, heads)
        state(h)
        send_head(0, u_send, u_recv, h)

    @pl.loop(0, heads)
    def _(h):
        c = cols(h)
        feat = features(mm(q_ref[:, c], w_ref[h], 1, 0))
        fq_s[:, c] = feat
        score = jnp.where(causal, mm(feat, fk_s[:, c], 1, 1), 0.0).astype(BF16)
        a_s[h] = score
        num_s[:, c] = mm(score, v_ref[:, c], 1, 0)

    def scan_up(j, acc):
        wait_chunk(0, u_recv, j)
        p_send[j] = acc.astype(BF16)
        return acc + u_recv[j].astype(F32)

    lax.fori_loop(0, n, scan_up, jnp.zeros((rows, dh), F32))

    @pl.loop(1, n + 1)
    def _(i):
        send_chunk(1, p_send, p_buf, lax.rem(me + i, n))

    @pl.loop(0, heads)
    def _(i):
        h = lax.rem(my_head + heads - i, heads)
        c = cols(h)
        wait_head(1, p_buf, h)
        num = num_s[:, c] + mm(fq_s[:, c], head_of(p_buf, h), 1, 0)
        recip = lax.rsqrt(jnp.mean(num * num, axis=-1, keepdims=True) + 1e-06)
        att_ref[:, c] = (num * recip).astype(BF16)
        y = y_ref[:, c].astype(F32)
        inner = jnp.mean(y * num, axis=-1, keepdims=True)
        g = (recip * (y - num * (recip * recip * inner))).astype(BF16)
        g_s[:, c] = g
        put_head(r_send, h, mm(fq_s[:, c], g, 0, 0))
        send_head(2, r_send, r_recv, h)

    @pl.loop(0, heads)
    def _(h):
        c = cols(h)
        g = g_s[:, c]
        back = jnp.where(causal, mm(g, v_ref[:, c], 1, 1), 0.0).astype(BF16)
        fq = fq_s[:, c]
        gfq = mm(back, fk_s[:, c], 1, 0) + mm(g, head_of(p_buf, h), 1, 1)
        ga = (gfq * slope_of(fq)).astype(BF16)
        qg_ref[:, c] = mm(ga, w_ref[h], 1, 1).astype(BF16)
        wt_s[h] = mm(q_ref[:, c], ga, 0, 0)
        gfk_s[:, c] = mm(back, fq, 0, 0)
        vgl_s[:, c] = mm(a_s[h], g, 0, 0)

    def scan_down(i, acc):
        j = n - 1 - i
        wait_chunk(2, r_recv, j)
        s_send[j] = acc.astype(BF16)
        return acc + r_recv[j].astype(F32)

    lax.fori_loop(0, n, scan_down, jnp.zeros((rows, dh), F32))

    @pl.loop(1, n + 1)
    def _(i):
        send_chunk(3, s_send, q_buf, lax.rem(me + i, n))

    @pl.loop(0, heads)
    def _(i):
        h = lax.rem(my_head + heads - i, heads)
        c = cols(h)
        wait_head(3, q_buf, h)
        suffix = head_of(q_buf, h)
        fk = fk_s[:, c]
        vg_ref[:, c] = (vgl_s[:, c] + mm(fk, suffix, 1, 0)).astype(BF16)
        gfk = gfk_s[:, c] + mm(v_ref[:, c], suffix, 1, 1)
        gb = (gfk * slope_of(fk)).astype(BF16)
        kg_ref[:, c] = mm(gb, w_ref[h], 1, 1).astype(BF16)
        put_head(f_send, h, wt_s[h] + mm(k_ref[:, c], gb, 0, 0))
        send_head(4, f_send, f_recv, h)

    def collect(j, acc):
        wait_chunk(4, f_recv, j)
        return acc + f_recv[j].astype(F32)

    fg_ref[...] = lax.fori_loop(0, n, collect, jnp.zeros((rows, dh), F32)) * scale

    for phase, buf in enumerate((u_send, p_send, r_send, s_send, f_send)):
        part = buf.at[pl.ds(0, n - 1)]
        pltpu.make_async_remote_copy(
            src_ref=part, dst_ref=part, send_sem=send_sems.at[phase], recv_sem=recv_sems.at[phase, 0],
            device_id={"seq": lax.rem(me + 1, n)}, device_id_type=MESH).wait_send()


def local(queries, keys, values, feature_map, out_grad):
    tokens, width = queries.shape
    heads, dh, _ = feature_map.shape
    n = lax.axis_size("seq")
    rows = heads * dh // n
    wide = jax.ShapeDtypeStruct((tokens, width), BF16)
    vmem = pl.BlockSpec(memory_space=pltpu.VMEM)
    hold = pltpu.VMEM((n, rows, dh), BF16)
    outs = pl.pallas_call(
        functools.partial(kernel, n, heads, dh, 1.0 / math.sqrt(tokens * n)),
        out_shape=(wide, wide, wide, wide, jax.ShapeDtypeStruct((rows, dh), F32)),
        in_specs=[vmem] * 5,
        out_specs=(vmem,) * 5,
        scratch_shapes=[
            pltpu.VMEM((tokens, width), BF16),
            pltpu.VMEM((tokens, width), BF16),
            pltpu.VMEM((heads, tokens, tokens), BF16),
            pltpu.VMEM((tokens, width), F32),
            pltpu.VMEM((tokens, width), F32),
            pltpu.VMEM((tokens, width), F32),
            pltpu.VMEM((heads, dh, dh), F32),
            pltpu.VMEM((tokens, width), BF16),
        ] + [hold] * 10 + [
            pltpu.SemaphoreType.DMA((5,)),
            pltpu.SemaphoreType.DMA((5, n)),
        ],
        compiler_params=pltpu.CompilerParams(
            collective_id=0, has_side_effects=True, vmem_limit_bytes=48 << 20),
        name="linear_attention",
    )(queries, keys, values, feature_map, out_grad)
    return outs[:4] + (outs[4].reshape(rows * dh),)


def solution(mesh):
    wide = P(("grp", "seq"), None)
    return jax.shard_map(
        local, mesh=mesh, in_specs=(wide, wide, wide, P(), wide),
        out_specs=(wide, wide, wide, wide, P(("grp", "seq"))), check_vma=False)
```

time: 364 us -> 85.7 us (0.24)
  waiting for transfers between devices: 258 us -> 0 us
  Pallas kernels: 0 us -> 78.1 us
  starting transfers between devices: 36.2 us -> 0 us
  matrix products: 22 us -> 0 us
  between operations: 15.1 us -> 0.65 us
  other arithmetic: 12.9 us -> 0 us
  local copies, waits for them, and re-layouts: 19.2 us -> 6.77 us
    ppermute x8 -> x0, waiting for transfers between devices: 175 us -> none  [shifted(): lax.ppermute(value, axis, [(source, source + steps) for source in range(i...]
    unnamed x2 -> x0, waiting for transfers between devices: 82.9 us -> none
    pallas_call x0 -> x1, Pallas kernels: none -> 78.1 us  [local(): pl.pallas_call(functools.partial(kernel, n, heads, dh, 1.0 / math.sqrt(to...]
    ppermute x8 -> x0, starting transfers between devices: 36.2 us -> none  [shifted(): lax.ppermute(value, axis, [(source, source + steps) for source in range(i...]
    dot_general x18 -> x0, matrix products: 22 us -> none  [the longest x2 3.8 us: features(): jnp.einsum('thd,hde->the', inputs, weight, preferred_element_type=jnp.flo...]
    unnamed x60 -> x9, local copies, waits for them, and re-layouts: 15 us -> 6.77 us
    convert_element_type x5 -> x0, other arithmetic: 7.63 us -> none  [the longest x2 2.54 us: features(): return (lifted, mapped.astype(jnp.bfloat16))]
    add x6 -> x0, other arithmetic: 5.24 us -> none  [the longest x3 3.9 us: later_sum(): running = running + shifted(running, 'seq', -(1 << level))]
  transfers between devices with their start and end apart: 9 -> 0, of which waited for: 9 -> 0; matrix products, arithmetic and copies ran while one was open for 8% -> 0% of each run, Pallas kernels for 0% -> 0%
where the time goes in v1:
time: 85.7 us; the launch traced here: 85.5 us
  Pallas kernels  78.1 us (91%)
  local copies, waits for them, and re-layouts  6.77 us (8%)
    pallas_call x1, Pallas kernels, local(): pl.pallas_call(functools.partial(kernel, n, heads, dh, 1.0 / math.sqrt(to...  78.1 us
    unnamed x9, local copies, waits for them, and re-layouts  6.77 us

profile of v1, /device:TPU:0, one launch (start us, length us, event | category | flops | bytes accessed | tf_op | source)
XLA Modules:
  0.0 85.5 jit_solution(15894751226253568472)
XLA Ops:
  0.6 0.0 copy-start
  0.6 1.2 %copy-done = bf16[256,2048]{1,0:T(8,128)(2,1)S(1)} copy-done((bf16[256,2048]{1,0:T(8,128)(2,1)S(1)}, bf16[256,2048]{1,0:T(8,128)(2,1)}, u32[]{:S(2)}) %copy-start) | copy-done | bytes 1048600
  1.9 0.0 copy-start.1
  1.9 1.0 %copy-done.1 = bf16[16,128,128]{2,1,0:T(8,128)(2,1)S(1)} copy-done((bf16[16,128,128]{2,1,0:T(8,128)(2,1)S(1)}, bf16[16,128,128]{2,1,0:T(8,128)(2,1)}, u32[]{:S(2)}) %copy-start.1) | copy-done | bytes 524312
  2.9 78.1 %linear_attention.1 = (bf16[256,2048]{1,0:T(8,128)(2,1)S(1)}, bf16[256,2048]{1,0:T(8,128)(2,1)S(1)}, bf16[256,2048]{1,0:T(8,128)(2,1)S(1)}, bf16[256,2048]{1,0:T(8,128)(2,1)S(1)}, f32[128,128]{1,0:T(8,128)S(1)}) custom-call(bf16[256,2048]{1,0:T(8,128)(2,1)S(1)} %copy-done, bf16[256,2048]{1,0:T(8,128)(2,1)} %k_ref.1, bf16[256,2048]{1,0:T(8,128)(2,1)} %v_ref.1, ...), custom_call_target="tpu_custom_call" | custom-call | tf_op jit(solution)/shard_map/linear_attention/pallas_call | solution.py:200
  81.0 1.0 %copy.15 = bf16[256,2048]{1,0:T(8,128)(2,1)} copy(bf16[256,2048]{1,0:T(8,128)(2,1)S(1)} %get-tuple-element.20) | data formatting | bytes 2097152
  82.0 1.0 %copy.16 = bf16[256,2048]{1,0:T(8,128)(2,1)} copy(bf16[256,2048]{1,0:T(8,128)(2,1)S(1)} %get-tuple-element.21) | data formatting | bytes 2097152
  83.0 1.0 %copy.17 = bf16[256,2048]{1,0:T(8,128)(2,1)} copy(bf16[256,2048]{1,0:T(8,128)(2,1)S(1)} %get-tuple-element.22) | data formatting | bytes 2097152
  83.9 1.0 %copy.18 = bf16[256,2048]{1,0:T(8,128)(2,1)} copy(bf16[256,2048]{1,0:T(8,128)(2,1)S(1)} %get-tuple-element.23) | data formatting | bytes 2097152
  84.9 0.6 copy.19
Async XLA Ops:
  0.6 1.2 %copy-start = (bf16[256,2048]{1,0:T(8,128)(2,1)S(1)}, bf16[256,2048]{1,0:T(8,128)(2,1)}, u32[]{:S(2)}) copy-start(bf16[256,2048]{1,0:T(8,128)(2,1)} %q_ref.1) | copy-start | bytes 3145732
  1.9 1.0 %copy-start.1 = (bf16[16,128,128]{2,1,0:T(8,128)(2,1)S(1)}, bf16[16,128,128]{2,1,0:T(8,128)(2,1)}, u32[]{:S(2)}) copy-start(bf16[16,128,128]{2,1,0:T(8,128)(2,1)} %w_ref.1) | copy-start | bytes 1572868

commit v2 on v1

v2 whole, which is shorter than its diff:
```python
import functools
import math

import jax
import jax.numpy as jnp
from jax import lax
from jax.experimental import pallas as pl
from jax.experimental.pallas import tpu as pltpu
from jax.sharding import PartitionSpec as P

MESH = pl.DeviceIdType.MESH
BF16 = jnp.bfloat16
F32 = jnp.float32
GROUP = 4


def mm(a, b, ca, cb):
    return lax.dot_general(a, b, (((ca,), (cb,)), ((), ())), preferred_element_type=F32)


def kernel(n, heads, dh, scale, q_ref, k_ref, v_ref, w_ref, y_ref,
           att_ref, qg_ref, kg_ref, vg_ref, fg_ref,
           fq_s, fk_s, a_s, num_s, gfk_s, vgl_s, wt_s, g_s,
           u_send, r_send, f_send, p_full, s_full,
           u_pair, u_tot, u_recv, p_send, p_chip, p_fwd,
           r_pair, r_tot, r_recv, s_send, s_chip, s_fwd,
           f_pair, f_tot, f_recv,
           pair_send_sems, pair_recv_sems, chip_send_sems, chip_recv_sems):
    me = lax.axis_index("seq")
    chips = n // 2
    chip, core = me // 2, lax.rem(me, 2)
    other = 1 - core
    rows = heads * dh // n
    groups = heads // GROUP
    span = chips // groups
    my_group = chip // span
    tokens = q_ref.shape[0]
    wide = GROUP * dh
    first_core = core == 0

    barrier = pltpu.get_barrier_semaphore()

    @pl.loop(0, chips - 1)
    def _(i):
        to = 2 * lax.rem(chip + 1 + i, chips) + core
        pl.semaphore_signal(barrier, inc=1, device_id={"seq": to}, device_id_type=MESH)

    pl.semaphore_signal(barrier, inc=1, device_id={"seq": 2 * chip + other}, device_id_type=MESH)

    causal = (lax.broadcasted_iota(jnp.int32, (tokens, tokens), 0)
              >= lax.broadcasted_iota(jnp.int32, (tokens, tokens), 1))

    def cols(g):
        return [pl.ds(pl.multiple_of(g * wide + k * dh, dh), dh) for k in range(GROUP)]

    def part(g):
        return pl.ds(g * span, span)

    def to_pair(phase, g, src, dst):
        return pltpu.make_async_remote_copy(
            src_ref=src, dst_ref=dst, send_sem=pair_send_sems.at[phase],
            recv_sem=pair_recv_sems.at[phase, g], device_id={"seq": 2 * chip + other}, device_id_type=MESH)

    def send_chip(phase, src, dst, c):
        @pl.when(c != chip)
        def _():
            pltpu.make_async_remote_copy(
                src_ref=src.at[c], dst_ref=dst.at[chip], send_sem=chip_send_sems.at[phase],
                recv_sem=chip_recv_sems.at[phase, chip], device_id={"seq": 2 * c + core},
                device_id_type=MESH).start()

        @pl.when(c == chip)
        def _():
            dst[chip] = src[chip]

    def wait_chip(phase, dst, c):
        @pl.when(c != chip)
        def _():
            pltpu.make_async_remote_copy(
                src_ref=dst.at[c], dst_ref=dst.at[c], send_sem=chip_send_sems.at[phase],
                recv_sem=chip_recv_sems.at[phase, c], device_id={"seq": 2 * c + core},
                device_id_type=MESH).wait_recv()

    def send_group(phase, src, dst, g):
        @pl.loop(0, span)
        def _(i):
            send_chip(phase, src, dst, g * span + lax.rem(chip + i, span))

    def wait_group(phase, dst, g):
        @pl.loop(0, span)
        def _(i):
            wait_chip(phase, dst, g * span + i)

    def share(phase, g, full, paired, values):
        full[part(g)] = jnp.concatenate([v.astype(BF16) for v in values], axis=0).reshape(span, 2, rows, dh)
        to_pair(phase, g, full.at[part(g), other], paired.at[part(g)]).start()

    def total(phase, chip_phase, g, full, paired, tot, recv):
        to_pair(phase, g, paired.at[part(g)], paired.at[part(g)]).wait_recv()
        tot[part(g)] = (full[part(g), core].astype(F32) + paired[part(g)].astype(F32)).astype(BF16)
        send_group(chip_phase, tot, recv, g)

    def scan(phase, next_phase, recv, send, landing, order):
        def step(i, acc):
            c = order(i)
            wait_chip(phase, recv, c)
            send[c] = acc.astype(BF16)
            return acc + recv[c].astype(F32)

        lax.fori_loop(0, chips, step, jnp.zeros((rows, dh), F32))

        @pl.loop(0, groups)
        def _(i):
            send_group(next_phase, send, landing, lax.rem(my_group + i, groups))

    def hand_out(chip_phase, phase, g, landing, full, paired, fwd, out, own_adds):
        wait_group(chip_phase, landing, g)
        base = landing[part(g)].astype(F32)
        mine = base + jnp.where(own_adds, paired[part(g)].astype(F32), 0.0)
        theirs = base + jnp.where(own_adds, 0.0, full[part(g), core].astype(F32))
        fwd[part(g)] = theirs.astype(BF16)
        to_pair(phase, g, fwd.at[part(g)], out.at[part(g), core]).start()
        out[part(g), core] = mine.astype(BF16)

    def receive(phase, g, fwd, out):
        to_pair(phase, g, fwd.at[part(g)], out.at[part(g), other]).wait_recv()

    def heads_of(buf, g):
        block = buf[part(g)].reshape(wide, dh)
        return [block[k * dh:(k + 1) * dh] for k in range(GROUP)]

    def weights(g):
        return [w_ref[g * GROUP + k] for k in range(GROUP)]

    def features(lifted):
        return jnp.where(lifted > 0, lifted + 1.0, jnp.exp(jnp.minimum(lifted, 0.0))).astype(BF16)

    def slope_of(feat):
        return jnp.minimum(feat.astype(F32), 1.0)

    def state(g):
        cs = cols(g)
        lifted = [mm(k_ref[:, c], w, 1, 0) for c, w in zip(cs, weights(g))]
        feats = [features(x) for x in lifted]
        sums = [mm(f, v_ref[:, c], 0, 0) for c, f in zip(cs, feats)]
        for c, f in zip(cs, feats):
            fk_s[:, c] = f
        return sums

    def up(i):
        return lax.rem(my_group + i, groups)

    def down(i):
        return lax.rem(my_group + groups - i, groups)

    sums = state(up(1))
    pl.semaphore_wait(barrier, chips)
    share(0, up(1), u_send, u_pair, sums)

    @pl.loop(2, groups + 1)
    def _(i):
        share(0, up(i), u_send, u_pair, state(up(i)))
        total(0, 0, up(i - 1), u_send, u_pair, u_tot, u_recv)

    total(0, 0, up(groups), u_send, u_pair, u_tot, u_recv)

    def local_part(g):
        cs = cols(g)
        lifted = [mm(q_ref[:, c], w, 1, 0) for c, w in zip(cs, weights(g))]
        feats = [features(x) for x in lifted]
        scores = [mm(f, fk_s[:, c], 1, 1) for c, f in zip(cs, feats)]
        scores = [jnp.where(causal, x, 0.0).astype(BF16) for x in scores]
        nums = [mm(x, v_ref[:, c], 1, 0) for c, x in zip(cs, scores)]
        for k, c in enumerate(cs):
            fq_s[:, c] = feats[k]
            a_s[g * GROUP + k] = scores[k]
            num_s[:, c] = nums[k]

    half = groups // 2
    pl.loop(0, half)(local_part)
    scan(0, 1, u_recv, p_send, p_chip, lambda i: i)
    pl.loop(half, groups)(local_part)

    hand_out(1, 1, down(0), p_chip, u_send, u_pair, p_fwd, p_full, core == 1)

    @pl.loop(0, groups)
    def _(i):
        @pl.when(i + 1 < groups)
        def _():
            hand_out(1, 1, down(i + 1), p_chip, u_send, u_pair, p_fwd, p_full, core == 1)

        g = down(i)
        cs = cols(g)
        receive(1, g, p_fwd, p_full)
        prefixes = heads_of(p_full, g)
        fqs = [fq_s[:, c] for c in cs]
        nums = [num_s[:, c] + mm(f, p, 1, 0) for c, f, p in zip(cs, fqs, prefixes)]
        recips = [lax.rsqrt(jnp.mean(x * x, axis=-1, keepdims=True) + 1e-06) for x in nums]
        ys = [y_ref[:, c].astype(F32) for c in cs]
        inners = [jnp.mean(y * x, axis=-1, keepdims=True) for y, x in zip(ys, nums)]
        grads = [(r * (y - x * (r * r * m))).astype(BF16) for r, y, x, m in zip(recips, ys, nums, inners)]
        sums = [mm(f, x, 0, 0) for f, x in zip(fqs, grads)]
        for c, x, r, gr in zip(cs, nums, recips, grads):
            att_ref[:, c] = (x * r).astype(BF16)
            g_s[:, c] = gr
        share(2, g, r_send, r_pair, sums)

        @pl.when(i > 0)
        def _():
            total(2, 2, down(i - 1), r_send, r_pair, r_tot, r_recv)

    total(2, 2, down(groups - 1), r_send, r_pair, r_tot, r_recv)

    def adjoint_part(g):
        cs = cols(g)
        grads = [g_s[:, c] for c in cs]
        ws = weights(g)
        prefixes = heads_of(p_full, g)
        backs = [mm(x, v_ref[:, c], 1, 1) for x, c in zip(grads, cs)]
        backs = [jnp.where(causal, x, 0.0).astype(BF16) for x in backs]
        gfqs = [mm(b, fk_s[:, c], 1, 0) + mm(x, p, 1, 1) for b, c, x, p in zip(backs, cs, grads, prefixes)]
        fqs = [fq_s[:, c] for c in cs]
        gas = [(x * slope_of(f)).astype(BF16) for x, f in zip(gfqs, fqs)]
        qgs = [mm(x, w, 1, 1).astype(BF16) for x, w in zip(gas, ws)]
        wts = [mm(q_ref[:, c], x, 0, 0) for c, x in zip(cs, gas)]
        gfks = [mm(b, f, 0, 0) for b, f in zip(backs, fqs)]
        vgls = [mm(a_s[g * GROUP + k], x, 0, 0) for k, x in enumerate(grads)]
        for k, c in enumerate(cs):
            qg_ref[:, c] = qgs[k]
            wt_s[g * GROUP + k] = wts[k]
            gfk_s[:, c] = gfks[k]
            vgl_s[:, c] = vgls[k]

    pl.loop(0, half)(adjoint_part)
    scan(2, 3, r_recv, s_send, s_chip, lambda i: chips - 1 - i)
    pl.loop(half, groups)(adjoint_part)

    hand_out(3, 3, down(0), s_chip, r_send, r_pair, s_fwd, s_full, first_core)

    @pl.loop(0, groups)
    def _(i):
        @pl.when(i + 1 < groups)
        def _():
            hand_out(3, 3, down(i + 1), s_chip, r_send, r_pair, s_fwd, s_full, first_core)

        g = down(i)
        cs = cols(g)
        receive(3, g, s_fwd, s_full)
        ws = weights(g)
        suffixes = heads_of(s_full, g)
        fks = [fk_s[:, c] for c in cs]
        gfks = [gfk_s[:, c] + mm(v_ref[:, c], s, 1, 1) for c, s in zip(cs, suffixes)]
        gbs = [(x * slope_of(f)).astype(BF16) for x, f in zip(gfks, fks)]
        wts = [wt_s[g * GROUP + k] + mm(k_ref[:, c], x, 0, 0) for k, (c, x) in enumerate(zip(cs, gbs))]
        share(4, g, f_send, f_pair, wts)
        vgs = [vgl_s[:, c] + mm(f, s, 1, 0) for c, f, s in zip(cs, fks, suffixes)]
        kgs = [mm(x, w, 1, 1) for x, w in zip(gbs, ws)]
        for c, a, b in zip(cs, vgs, kgs):
            vg_ref[:, c] = a.astype(BF16)
            kg_ref[:, c] = b.astype(BF16)
        total(4, 4, g, f_send, f_pair, f_tot, f_recv)

    def collect(c, acc):
        wait_chip(4, f_recv, c)
        return acc + f_recv[c].astype(F32)

    fg_ref[...] = lax.fori_loop(0, chips, collect, jnp.zeros((rows, dh), F32)) * scale

    for phase, buf in enumerate((u_tot, p_send, r_tot, s_send, f_tot)):
        some = buf.at[pl.ds(0, chips - 1)]
        pltpu.make_async_remote_copy(
            src_ref=some, dst_ref=some, send_sem=chip_send_sems.at[phase], recv_sem=chip_recv_sems.at[phase, 0],
            device_id={"seq": 2 * chip + other}, device_id_type=MESH).wait_send()
        to_pair(phase, 0, buf, buf).wait_send()


def local(queries, keys, values, feature_map, out_grad):
    tokens, width = queries.shape
    heads, dh, _ = feature_map.shape
    n = lax.axis_size("seq")
    chips, groups = n // 2, heads // GROUP
    rows = heads * dh // n
    wide = jax.ShapeDtypeStruct((tokens, width), BF16)
    vmem = pl.BlockSpec(memory_space=pltpu.VMEM)
    outs = pl.pallas_call(
        functools.partial(kernel, n, heads, dh, 1.0 / math.sqrt(tokens * n)),
        out_shape=(wide, wide, wide, wide, jax.ShapeDtypeStruct((rows, dh), F32)),
        in_specs=[vmem] * 5,
        out_specs=(vmem,) * 5,
        scratch_shapes=[
            pltpu.VMEM((tokens, width), BF16),
            pltpu.VMEM((tokens, width), BF16),
            pltpu.VMEM((heads, tokens, tokens), BF16),
            pltpu.VMEM((tokens, width), F32),
            pltpu.VMEM((tokens, width), F32),
            pltpu.VMEM((tokens, width), F32),
            pltpu.VMEM((heads, dh, dh), F32),
            pltpu.VMEM((tokens, width), BF16),
        ] + [pltpu.VMEM((chips, 2, rows, dh), BF16)] * 5 + [pltpu.VMEM((chips, rows, dh), BF16)] * 15 + [
            pltpu.SemaphoreType.DMA((5,)),
            pltpu.SemaphoreType.DMA((5, groups)),
            pltpu.SemaphoreType.DMA((5,)),
            pltpu.SemaphoreType.DMA((5, chips)),
        ],
        compiler_params=pltpu.CompilerParams(
            collective_id=0, has_side_effects=True, vmem_limit_bytes=48 << 20),
        name="linear_attention",
    )(queries, keys, values, feature_map, out_grad)
    return outs[:4] + (outs[4].reshape(rows * dh),)


def solution(mesh):
    wide = P(("grp", "seq"), None)
    return jax.shard_map(
        local, mesh=mesh, in_specs=(wide, wide, wide, P(), wide),
        out_specs=(wide, wide, wide, wide, P(("grp", "seq"))), check_vma=False)
```

time: 85.7 us -> 58 us (0.68)
  Pallas kernels: 78.1 us -> 50.4 us
    pallas_call x1, Pallas kernels: 78.1 us -> 50.4 us  [local(): pl.pallas_call(functools.partial(kernel, n, heads, dh, 1.0 / math.sqrt(to...]
where the time goes in v2:
time: 58 us; the launch traced here: 57.8 us
  Pallas kernels  50.4 us (87%)
  local copies, waits for them, and re-layouts  6.77 us (12%)
  between operations  0.65 us (1%)
    pallas_call x1, Pallas kernels, local(): pl.pallas_call(functools.partial(kernel, n, heads, dh, 1.0 / math.sqrt(to...  50.4 us
    unnamed x9, local copies, waits for them, and re-layouts  6.77 us

profile of v2, /device:TPU:0, one launch (start us, length us, event | category | flops | bytes accessed | tf_op | source)
XLA Modules:
  0.0 57.8 jit_solution(4442643350308288295)
XLA Ops:
  0.6 0.0 copy-start
  0.6 1.2 %copy-done = bf16[256,2048]{1,0:T(8,128)(2,1)S(1)} copy-done((bf16[256,2048]{1,0:T(8,128)(2,1)S(1)}, bf16[256,2048]{1,0:T(8,128)(2,1)}, u32[]{:S(2)}) %copy-start) | copy-done | bytes 1048600
  1.9 0.0 copy-start.1
  1.9 1.0 %copy-done.1 = bf16[16,128,128]{2,1,0:T(8,128)(2,1)S(1)} copy-done((bf16[16,128,128]{2,1,0:T(8,128)(2,1)S(1)}, bf16[16,128,128]{2,1,0:T(8,128)(2,1)}, u32[]{:S(2)}) %copy-start.1) | copy-done | bytes 524312
  2.9 50.4 %linear_attention.1 = (bf16[256,2048]{1,0:T(8,128)(2,1)S(1)}, bf16[256,2048]{1,0:T(8,128)(2,1)S(1)}, bf16[256,2048]{1,0:T(8,128)(2,1)S(1)}, bf16[256,2048]{1,0:T(8,128)(2,1)S(1)}, f32[128,128]{1,0:T(8,128)S(1)}) custom-call(bf16[256,2048]{1,0:T(8,128)(2,1)S(1)} %copy-done, bf16[256,2048]{1,0:T(8,128)(2,1)} %k_ref.1, bf16[256,2048]{1,0:T(8,128)(2,1)} %v_ref.1, ...), custom_call_target="tpu_custom_call" | custom-call | tf_op jit(solution)/shard_map/linear_attention/pallas_call | solution.py:285
  53.3 1.0 %copy.15 = bf16[256,2048]{1,0:T(8,128)(2,1)} copy(bf16[256,2048]{1,0:T(8,128)(2,1)S(1)} %get-tuple-element.20) | data formatting | bytes 2097152
  54.3 1.0 %copy.16 = bf16[256,2048]{1,0:T(8,128)(2,1)} copy(bf16[256,2048]{1,0:T(8,128)(2,1)S(1)} %get-tuple-element.21) | data formatting | bytes 2097152
  55.3 1.0 %copy.17 = bf16[256,2048]{1,0:T(8,128)(2,1)} copy(bf16[256,2048]{1,0:T(8,128)(2,1)S(1)} %get-tuple-element.22) | data formatting | bytes 2097152
  56.2 1.0 %copy.18 = bf16[256,2048]{1,0:T(8,128)(2,1)} copy(bf16[256,2048]{1,0:T(8,128)(2,1)S(1)} %get-tuple-element.23) | data formatting | bytes 2097152
  57.2 0.6 %copy.19 = f32[16384]{0:T(1024)} copy(f32[16384]{0:T(1024)S(1)} %bitcast.1) | data formatting | bytes 131072
Async XLA Ops:
  0.6 1.2 %copy-start = (bf16[256,2048]{1,0:T(8,128)(2,1)S(1)}, bf16[256,2048]{1,0:T(8,128)(2,1)}, u32[]{:S(2)}) copy-start(bf16[256,2048]{1,0:T(8,128)(2,1)} %q_ref.1) | copy-start | bytes 3145732
  1.9 1.0 %copy-start.1 = (bf16[16,128,128]{2,1,0:T(8,128)(2,1)S(1)}, bf16[16,128,128]{2,1,0:T(8,128)(2,1)}, u32[]{:S(2)}) copy-start(bf16[16,128,128]{2,1,0:T(8,128)(2,1)} %w_ref.1) | copy-start | bytes 1572868

commit v3 on v2

--- a/solution.py
+++ b/solution.py
@@ -12,20 +12,22 @@
 BF16 = jnp.bfloat16
 F32 = jnp.float32
 GROUP = 4
+PIECES = 2
 
 
 def mm(a, b, ca, cb):
     return lax.dot_general(a, b, (((ca,), (cb,)), ((), ())), preferred_element_type=F32)
 
 
-def kernel(n, heads, dh, scale, q_ref, k_ref, v_ref, w_ref, y_ref,
-           att_ref, qg_ref, kg_ref, vg_ref, fg_ref,
-           fq_s, fk_s, a_s, num_s, gfk_s, vgl_s, wt_s, g_s,
+def kernel(n, heads, dh, scale, q_hbm, k_hbm, v_hbm, w_hbm, y_hbm,
+           att_hbm, qg_hbm, kg_hbm, vg_hbm, fg_ref,
+           q_ref, k_ref, v_ref, w_ref, y_ref, att_ref, qg_ref, kg_ref, vg_ref,
+           fq_s, fk_s, gb_s, a_s, num_s, gfk_s, vgl_s, wt_s, g_s,
            u_send, r_send, f_send, p_full, s_full,
            u_pair, u_tot, u_recv, p_send, p_chip, p_fwd,
            r_pair, r_tot, r_recv, s_send, s_chip, s_fwd,
            f_pair, f_tot, f_recv,
-           pair_send_sems, pair_recv_sems, chip_send_sems, chip_recv_sems):
+           pair_send_sems, pair_recv_sems, chip_send_sems, chip_recv_sems, load_sems, late_sems, out_sems):
     me = lax.axis_index("seq")
     chips = n // 2
     chip, core = me // 2, lax.rem(me, 2)
@@ -36,6 +38,30 @@
     my_group = chip // span
     tokens = q_ref.shape[0]
     wide = GROUP * dh
+
+    def loads(g):
+        some = pl.ds(pl.multiple_of(g * wide, wide), wide)
+        some_heads = pl.ds(g * GROUP, GROUP)
+        return (
+            pltpu.make_async_copy(w_hbm.at[some_heads], w_ref.at[some_heads], load_sems.at[0, g]),
+            pltpu.make_async_copy(k_hbm.at[:, some], k_ref.at[:, some], load_sems.at[1, g]),
+            pltpu.make_async_copy(v_hbm.at[:, some], v_ref.at[:, some], load_sems.at[2, g]),
+        )
+
+    def store(which, g):
+        some = pl.ds(pl.multiple_of(g * wide, wide), wide)
+        src, dst = ((att_ref, att_hbm), (qg_ref, qg_hbm), (kg_ref, kg_hbm), (vg_ref, vg_hbm))[which]
+        return pltpu.make_async_copy(src.at[:, some], dst.at[:, some], out_sems.at[which, g])
+
+    @pl.loop(1, groups + 1)
+    def _(i):
+        for copy in loads(lax.rem(my_group + i, groups)):
+            copy.start()
+
+    load_q = pltpu.make_async_copy(q_hbm, q_ref, late_sems.at[0])
+    load_y = pltpu.make_async_copy(y_hbm, y_ref, late_sems.at[1])
+    load_q.start()
+    load_y.start()
     first_core = core == 0
 
     barrier = pltpu.get_barrier_semaphore()
@@ -139,6 +165,8 @@
         return jnp.minimum(feat.astype(F32), 1.0)
 
     def state(g):
+        for copy in loads(g):
+            copy.wait()
         cs = cols(g)
         lifted = [mm(k_ref[:, c], w, 1, 0) for c, w in zip(cs, weights(g))]
         feats = [features(x) for x in lifted]
@@ -177,10 +205,12 @@
             num_s[:, c] = nums[k]
 
     half = groups // 2
+    load_q.wait()
     pl.loop(0, half)(local_part)
     scan(0, 1, u_recv, p_send, p_chip, lambda i: i)
     pl.loop(half, groups)(local_part)
 
+    load_y.wait()
     hand_out(1, 1, down(0), p_chip, u_send, u_pair, p_fwd, p_full, core == 1)
 
     @pl.loop(0, groups)
@@ -203,6 +233,7 @@
         for c, x, r, gr in zip(cs, nums, recips, grads):
             att_ref[:, c] = (x * r).astype(BF16)
             g_s[:, c] = gr
+        store(0, g).start()
         share(2, g, r_send, r_pair, sums)
 
         @pl.when(i > 0)
@@ -230,6 +261,7 @@
             wt_s[g * GROUP + k] = wts[k]
             gfk_s[:, c] = gfks[k]
             vgl_s[:, c] = vgls[k]
+        store(1, g).start()
 
     pl.loop(0, half)(adjoint_part)
     scan(2, 3, r_recv, s_send, s_chip, lambda i: chips - 1 - i)
@@ -246,25 +278,43 @@
         g = down(i)
         cs = cols(g)
         receive(3, g, s_fwd, s_full)
-        ws = weights(g)
         suffixes = heads_of(s_full, g)
         fks = [fk_s[:, c] for c in cs]
         gfks = [gfk_s[:, c] + mm(v_ref[:, c], s, 1, 1) for c, s in zip(cs, suffixes)]
         gbs = [(x * slope_of(f)).astype(BF16) for x, f in zip(gfks, fks)]
         wts = [wt_s[g * GROUP + k] + mm(k_ref[:, c], x, 0, 0) for k, (c, x) in enumerate(zip(cs, gbs))]
+        for c, x in zip(cs, gbs):
+            gb_s[:, c] = x
         share(4, g, f_send, f_pair, wts)
-        vgs = [vgl_s[:, c] + mm(f, s, 1, 0) for c, f, s in zip(cs, fks, suffixes)]
-        kgs = [mm(x, w, 1, 1) for x, w in zip(gbs, ws)]
+
+        @pl.when(i > 0)
+        def _():
+            total(4, 4, down(i - 1), f_send, f_pair, f_tot, f_recv)
+
+    total(4, 4, down(groups - 1), f_send, f_pair, f_tot, f_recv)
+
+    @pl.loop(0, groups)
+    def _(g):
+        cs = cols(g)
+        suffixes = heads_of(s_full, g)
+        vgs = [vgl_s[:, c] + mm(fk_s[:, c], s, 1, 0) for c, s in zip(cs, suffixes)]
+        kgs = [mm(gb_s[:, c], w, 1, 1) for c, w in zip(cs, weights(g))]
         for c, a, b in zip(cs, vgs, kgs):
             vg_ref[:, c] = a.astype(BF16)
             kg_ref[:, c] = b.astype(BF16)
-        total(4, 4, g, f_send, f_pair, f_tot, f_recv)
+        store(2, g).start()
+        store(3, g).start()
 
     def collect(c, acc):
         wait_chip(4, f_recv, c)
         return acc + f_recv[c].astype(F32)
 
     fg_ref[...] = lax.fori_loop(0, chips, collect, jnp.zeros((rows, dh), F32)) * scale
+
+    @pl.loop(0, groups)
+    def _(g):
+        for which in range(4):
+            store(which, g).wait()
 
     for phase, buf in enumerate((u_tot, p_send, r_tot, s_send, f_tot)):
         some = buf.at[pl.ds(0, chips - 1)]
@@ -272,6 +322,30 @@
             src_ref=some, dst_ref=some, send_sem=chip_send_sems.at[phase], recv_sem=chip_recv_sems.at[phase, 0],
             device_id={"seq": 2 * chip + other}, device_id_type=MESH).wait_send()
         to_pair(phase, 0, buf, buf).wait_send()
+
+
+def copy_out(*refs):
+    ins, outs, held = refs[:5], refs[5:10], refs[10:15]
+    in_sems, out_sems = refs[15:]
+
+    def parts(sources, targets, sems):
+        copies = []
+        for i, (source, target) in enumerate(zip(sources, targets)):
+            size = source.shape[0] // PIECES
+            for p in range(PIECES):
+                some = pl.ds(p * size, size)
+                copies.append(pltpu.make_async_copy(source.at[some], target.at[some], sems.at[i, p]))
+        return copies
+
+    reads = parts(ins, held, in_sems)
+    writes = parts(held, outs, out_sems)
+    for read in reads:
+        read.start()
+    for read, write in zip(reads, writes):
+        read.wait()
+        write.start()
+    for write in writes:
+        write.wait()
 
 
 def local(queries, keys, values, feature_map, out_grad):
@@ -282,14 +356,15 @@
     rows = heads * dh // n
     wide = jax.ShapeDtypeStruct((tokens, width), BF16)
     vmem = pl.BlockSpec(memory_space=pltpu.VMEM)
+    hbm = pl.BlockSpec(memory_space=pltpu.HBM)
+    shapes = (wide, wide, wide, wide, jax.ShapeDtypeStruct((rows, dh), F32))
     outs = pl.pallas_call(
         functools.partial(kernel, n, heads, dh, 1.0 / math.sqrt(tokens * n)),
-        out_shape=(wide, wide, wide, wide, jax.ShapeDtypeStruct((rows, dh), F32)),
-        in_specs=[vmem] * 5,
-        out_specs=(vmem,) * 5,
-        scratch_shapes=[
-            pltpu.VMEM((tokens, width), BF16),
-            pltpu.VMEM((tokens, width), BF16),
+        out_shape=shapes,
+        in_specs=[hbm] * 5,
+        out_specs=(hbm,) * 4 + (vmem,),
+        scratch_shapes=[pltpu.VMEM((tokens, width), BF16)] * 3 + [pltpu.VMEM((heads, dh, dh), BF16)] + [
+            pltpu.VMEM((tokens, width), BF16)] * 8 + [
             pltpu.VMEM((heads, tokens, tokens), BF16),
             pltpu.VMEM((tokens, width), F32),
             pltpu.VMEM((tokens, width), F32),
@@ -301,12 +376,24 @@
             pltpu.SemaphoreType.DMA((5, groups)),
             pltpu.SemaphoreType.DMA((5,)),
             pltpu.SemaphoreType.DMA((5, chips)),
+            pltpu.SemaphoreType.DMA((3, groups)),
+            pltpu.SemaphoreType.DMA((2,)),
+            pltpu.SemaphoreType.DMA((4, groups)),
         ],
         compiler_params=pltpu.CompilerParams(
-            collective_id=0, has_side_effects=True, vmem_limit_bytes=48 << 20),
+            collective_id=0, has_side_effects=True, vmem_limit_bytes=56 << 20),
         name="linear_attention",
     )(queries, keys, values, feature_map, out_grad)
-    return outs[:4] + (outs[4].reshape(rows * dh),)
+    outs = pl.pallas_call(
+        copy_out,
+        out_shape=shapes,
+        in_specs=[hbm] * 5,
+        out_specs=(hbm,) * 5,
+        scratch_shapes=[pltpu.VMEM(x.shape, x.dtype) for x in shapes] + [pltpu.SemaphoreType.DMA((5, PIECES))] * 2,
+        compiler_params=pltpu.CompilerParams(vmem_limit_bytes=56 << 20),
+        name="copy_out",
+    )(*outs)
+    return tuple(outs[:4]) + (outs[4].reshape(rows * dh),)
 
 
 def solution(mesh):

time: 58 us -> 55.1 us (0.950)
  local copies, waits for them, and re-layouts: 6.77 us -> 0 us
  Pallas kernels: 50.4 us -> 54.3 us
    unnamed x9 -> x0, local copies, waits for them, and re-layouts: 6.77 us -> none
    pallas_call x0 -> x1, Pallas kernels: none -> 3.62 us  [local(): pl.pallas_call(copy_out, out_shape=shapes, in_specs=[hbm] * 5, out_specs=...]
where the time goes in v3:
time: 55.1 us; the launch traced here: 54.9 us
  Pallas kernels  54.3 us (99%)
  between operations  0.64 us (1%)
    pallas_call x1, Pallas kernels, local(): pl.pallas_call(functools.partial(kernel, n, heads, dh, 1.0 / math.sqrt(to...  50.7 us
    pallas_call x1, Pallas kernels, local(): pl.pallas_call(copy_out, out_shape=shapes, in_specs=[hbm] * 5, out_specs=...  3.62 us

profile of v3, /device:TPU:0, one launch (start us, length us, event | category | flops | bytes accessed | tf_op | source)
XLA Modules:
  0.0 54.9 jit_solution(13275231067052411386)
XLA Ops:
  0.6 50.7 %linear_attention.1 = (bf16[256,2048]{1,0:T(8,128)(2,1)}, bf16[256,2048]{1,0:T(8,128)(2,1)}, bf16[256,2048]{1,0:T(8,128)(2,1)}, bf16[256,2048]{1,0:T(8,128)(2,1)}, f32[128,128]{1,0:T(8,128)}) custom-call(bf16[256,2048]{1,0:T(8,128)(2,1)} %q_hbm.1, bf16[256,2048]{1,0:T(8,128)(2,1)} %k_hbm.1, bf16[256,2048]{1,0:T(8,128)(2,1)} %v_hbm.1, ...), custom_call_target="tpu_custom_call" | custom-call | tf_op jit(solution)/shard_map/linear_attention/pallas_call | solution.py:361
  51.3 3.6 %copy_out.1 = (bf16[256,2048]{1,0:T(8,128)(2,1)}, bf16[256,2048]{1,0:T(8,128)(2,1)}, bf16[256,2048]{1,0:T(8,128)(2,1)}, bf16[256,2048]{1,0:T(8,128)(2,1)}, f32[128,128]{1,0:T(8,128)}) custom-call(bf16[256,2048]{1,0:T(8,128)(2,1)} %get-tuple-element.15.refs_0_, bf16[256,2048]{1,0:T(8,128)(2,1)} %get-tuple-element.16.refs_1_, ...), custom_call_target="tpu_custom_call" | custom-call | tf_op jit(solution)/shard_map/copy_out/pallas_call | solution.py:387

commit v4 on v3

--- a/solution.py
+++ b/solution.py
@@ -12,7 +12,7 @@
 BF16 = jnp.bfloat16
 F32 = jnp.float32
 GROUP = 4
-PIECES = 2
+PIECES = 1
 
 
 def mm(a, b, ca, cb):
@@ -108,12 +108,12 @@
                 device_id_type=MESH).wait_recv()
 
     def send_group(phase, src, dst, g):
-        @pl.loop(0, span)
+        @pl.loop(0, span, unroll=span <= 8)
         def _(i):
             send_chip(phase, src, dst, g * span + lax.rem(chip + i, span))
 
     def wait_group(phase, dst, g):
-        @pl.loop(0, span)
+        @pl.loop(0, span, unroll=span <= 8)
         def _(i):
             wait_chip(phase, dst, g * span + i)
 
@@ -133,9 +133,9 @@
             send[c] = acc.astype(BF16)
             return acc + recv[c].astype(F32)
 
-        lax.fori_loop(0, chips, step, jnp.zeros((rows, dh), F32))
-
-        @pl.loop(0, groups)
+        lax.fori_loop(0, chips, step, jnp.zeros((rows, dh), F32), unroll=chips <= 8)
+
+        @pl.loop(0, groups, unroll=chips <= 8)
         def _(i):
             send_group(next_phase, send, landing, lax.rem(my_group + i, groups))
 
@@ -309,7 +309,7 @@
         wait_chip(4, f_recv, c)
         return acc + f_recv[c].astype(F32)
 
-    fg_ref[...] = lax.fori_loop(0, chips, collect, jnp.zeros((rows, dh), F32)) * scale
+    fg_ref[...] = lax.fori_loop(0, chips, collect, jnp.zeros((rows, dh), F32), unroll=chips <= 8) * scale
 
     @pl.loop(0, groups)
     def _(g):

time: 55.1 us -> 54.7 us (level)
  no operation moved by 1% of the time
where the time goes in v4:
time: 54.7 us; the launch traced here: 54.5 us
  Pallas kernels  53.9 us (99%)
  between operations  0.64 us (1%)
    pallas_call x1, Pallas kernels, local(): pl.pallas_call(functools.partial(kernel, n, heads, dh, 1.0 / math.sqrt(to...  50.6 us
    pallas_call x1, Pallas kernels, local(): pl.pallas_call(copy_out, out_shape=shapes, in_specs=[hbm] * 5, out_specs=...  3.32 us

profile of v4, /device:TPU:0, one launch (start us, length us, event | category | flops | bytes accessed | tf_op | source)
XLA Modules:
  0.0 54.5 jit_solution(12900995961586983526)
XLA Ops:
  0.6 50.6 %linear_attention.1 = (bf16[256,2048]{1,0:T(8,128)(2,1)}, bf16[256,2048]{1,0:T(8,128)(2,1)}, bf16[256,2048]{1,0:T(8,128)(2,1)}, bf16[256,2048]{1,0:T(8,128)(2,1)}, f32[128,128]{1,0:T(8,128)}) custom-call(bf16[256,2048]{1,0:T(8,128)(2,1)} %q_hbm.1, bf16[256,2048]{1,0:T(8,128)(2,1)} %k_hbm.1, bf16[256,2048]{1,0:T(8,128)(2,1)} %v_hbm.1, ...), custom_call_target="tpu_custom_call" | custom-call | tf_op jit(solution)/shard_map/linear_attention/pallas_call | solution.py:361
  51.2 3.3 %copy_out.1 = (bf16[256,2048]{1,0:T(8,128)(2,1)}, bf16[256,2048]{1,0:T(8,128)(2,1)}, bf16[256,2048]{1,0:T(8,128)(2,1)}, bf16[256,2048]{1,0:T(8,128)(2,1)}, f32[128,128]{1,0:T(8,128)}) custom-call(bf16[256,2048]{1,0:T(8,128)(2,1)} %get-tuple-element.15.refs_0_, bf16[256,2048]{1,0:T(8,128)(2,1)} %get-tuple-element.16.refs_1_, ...), custom_call_target="tpu_custom_call" | custom-call | tf_op jit(solution)/shard_map/copy_out/pallas_call | solution.py:387
